TPU v7x, 512 devices: a whole 4x4x16 slice. The times are simulated.
512 devices in a mesh: row: 8 (over y, core), col: 16 (over z), ch: 4 (over x).
Axes of the slice: x: 4, y: 4, z: 16, core: 2. Of those that a mesh axis runs over, the one named last changes fastest.
Arguments:
- image: bfloat16 [256, 32, 2048], P('ch', 'row', 'col'), may hold values from -6 to 6
- depth_kernel: float32 [256, 49], P('ch'), may hold values from -0.875 to 0.875
- norm_gain: float32 [256], P('ch'), may hold values from 0.25 to 1.75
- norm_shift: float32 [256], P('ch'), may hold values from -3 to 3
- expand_weight: bfloat16 [256, 1024], P(None, 'ch'), may hold values from -0.375 to 0.375
- expand_bias: float32 [1024], replicated, may hold values from -3 to 3
- reduce_weight: bfloat16 [1024, 256], P('ch'), may hold values from -0.1875 to 0.1875
- cotangent: bfloat16 [256, 32, 2048], P('ch', 'row', 'col'), may hold values from -6 to 6
Outputs:
- result: bfloat16 [256, 32, 2048], P('ch', 'row', 'col')
- grad_image: bfloat16 [256, 32, 2048], P('ch', 'row', 'col')
- grad_kernel: float32 [256, 49], P('ch')
- grad_gain: float32 [256], P('ch')
- grad_shift: float32 [256], P('ch')
- grad_expand: float32 [256, 1024], P(None, 'ch')
- grad_offset: float32 [1024], P('ch')
- grad_reduce: float32 [1024, 256], P('ch')
All inputs are finite; a program needn't handle non-finite values.
Results may differ from a plain program's by a relative error of at most 0.011.
Values may be sent and summed in bfloat16 or wider, within the bound.
No kernel may reach another device: no remote copies, remote signals or barrier semaphores. Data moves between devices by JAX's collectives and lax.ppermute only.
A program may use at most 64 MiB of HBM per device.

v0:
```python
import jax
import jax.numpy as jnp
from jax import lax
from jax.sharding import PartitionSpec as P

KSIZE = 7
epsilon = 1e-06
root_two_pi = 0.7978845608028654
cubic_coef = 0.044715


def padded_2(x, sides, width):
    for axis, dim in sides:
        size, length = (lax.axis_size(axis), x.shape[dim])
        up = [(i, (i + 1) % size) for i in range(size - 1)]
        down = [(j, i) for i, j in up]
        last = lax.slice_in_dim(x, length - width, length, axis=dim)
        leading = lax.slice_in_dim(x, 0, width, axis=dim)
        before = lax.ppermute(last, axis, up)
        after = lax.ppermute(leading, axis, down)
        x = jnp.concatenate([before, x, after], axis=dim)
    return x


def product(left, right, dims):
    return lax.dot_general(
        left.astype(jnp.float32),
        right.astype(jnp.float32),
        dims,
        preferred_element_type=jnp.float32,
    )


def gelu_pair(hidden):
    inner = root_two_pi * (hidden + cubic_coef * hidden * hidden * hidden)
    tangent = jnp.tanh(inner)
    value = 0.5 * hidden * (1.0 + tangent)
    slope = 0.5 * (1.0 + tangent) + 0.5 * hidden * (1.0 - tangent * tangent) * root_two_pi * (
        1.0 + 3.0 * cubic_coef * hidden * hidden
    )
    return (value, slope)


def tap_window(padded, kernel, tap, first, second, tile_rows, tile_cols):
    window = lax.dynamic_slice(
        padded, (jnp.int32(0), first, second), (padded.shape[0], tile_rows, tile_cols)
    )
    weight = lax.dynamic_slice_in_dim(kernel, tap, 1, 1)
    return weight[:, :, None] * window


def forward_taps(padded, kernel, span, tile_rows, tile_cols):

    def forward_step(tap, accum):
        tap = jnp.asarray(tap).astype(jnp.int32)
        first = tap // span
        second = tap % span
        return accum + tap_window(padded, kernel, tap, first, second, tile_rows, tile_cols)

    accum = jnp.zeros((padded.shape[0], tile_rows, tile_cols), jnp.float32)
    return lax.fori_loop(0, span * span, forward_step, accum)


def backward_taps(padded, kernel, span, tile_rows, tile_cols):
    reach = span - 1

    def backward_step(tap, accum):
        tap = jnp.asarray(tap).astype(jnp.int32)
        first = reach - tap // span
        second = reach - tap % span
        return accum + tap_window(padded, kernel, tap, first, second, tile_rows, tile_cols)

    accum = jnp.zeros((padded.shape[0], tile_rows, tile_cols), jnp.float32)
    return lax.fori_loop(0, span * span, backward_step, accum)


def kernel_grad(grad_mixed, padded, span, tile_rows, tile_cols):

    def kernel_step(tap, table):
        tap = jnp.asarray(tap).astype(jnp.int32)
        first = tap // span
        second = tap % span
        window = lax.dynamic_slice(
            padded, (jnp.int32(0), first, second), (padded.shape[0], tile_rows, tile_cols)
        )
        column = jnp.sum(grad_mixed * window, axis=(1, 2))
        return lax.dynamic_update_slice_in_dim(table, column[:, None], tap, 1)

    table = jnp.zeros((grad_mixed.shape[0], span * span), jnp.float32)
    return lax.fori_loop(0, span * span, kernel_step, table)


def body(
    image, depth_kernel, norm_gain, norm_shift, expand_weight, expand_bias, reduce_weight, cotangent
):
    channels, tile_rows, tile_cols = image.shape
    pixels = tile_rows * tile_cols
    all_channels = channels * lax.axis_size("ch")
    hid_local = reduce_weight.shape[0]
    half = KSIZE // 2
    padded = padded_2(image, (("row", 1), ("col", 2)), half).astype(jnp.float32)
    mixed = forward_taps(padded, depth_kernel, KSIZE, tile_rows, tile_cols)
    flat_cot = cotangent.reshape(channels, pixels)
    contract_first = (((0,), (0,)), ((), ()))
    contract_last = (((1,), (1,)), ((), ()))
    plain = (((1,), (0,)), ((), ()))
    centre = lax.psum(jnp.sum(mixed, axis=0), "ch") / all_channels
    diff = mixed - centre
    variance = lax.psum(jnp.sum(diff * diff, axis=0), "ch") / all_channels
    inverse = lax.rsqrt(variance + epsilon)
    normed = diff * inverse
    normal = (normed * norm_gain[:, None, None] + norm_shift[:, None, None]).astype(jnp.bfloat16)
    flat_normal = normal.reshape(channels, pixels)
    bias_local = lax.dynamic_slice_in_dim(expand_bias, lax.axis_index("ch") * hid_local, hid_local)
    full_normal = lax.all_gather(flat_normal, "ch", axis=0, tiled=True)
    hidden = product(expand_weight, full_normal, contract_first) + bias_local[:, None]
    value, slope = gelu_pair(hidden)
    active = value.astype(jnp.bfloat16)
    mlp_local = lax.psum_scatter(
        product(reduce_weight, active, contract_first), "ch", scatter_dimension=0, tiled=True
    )
    full_cot = lax.all_gather(flat_cot, "ch", axis=0, tiled=True)
    grad_act = product(reduce_weight, full_cot, plain)
    grad_hidden = (grad_act * slope).astype(jnp.bfloat16)
    grad_red = product(active, full_cot, contract_last)
    grad_exp = product(full_normal, grad_hidden, contract_last)
    grad_off = jnp.sum(grad_hidden.astype(jnp.float32), axis=1)
    grad_local = lax.psum_scatter(
        product(expand_weight, grad_hidden, plain).astype(jnp.bfloat16),
        "ch",
        scatter_dimension=0,
        tiled=True,
    ).astype(jnp.float32)
    grad_normal = grad_local.reshape(channels, tile_rows, tile_cols)
    grad_normed = grad_normal * norm_gain[:, None, None]
    plain_sum, cross_sum = lax.psum(
        (jnp.sum(grad_normed, axis=0), jnp.sum(grad_normed * normed, axis=0)), "ch"
    )
    grad_gain = jnp.sum(grad_normal * normed, axis=(1, 2))
    grad_shift = jnp.sum(grad_normal, axis=(1, 2))
    grad_mixed = inverse * (
        grad_normed - plain_sum / all_channels - normed * (cross_sum / all_channels)
    )
    result = (image.astype(jnp.float32) + mlp_local.reshape(channels, tile_rows, tile_cols)).astype(
        jnp.bfloat16
    )
    grad_pad = padded_2(grad_mixed.astype(jnp.bfloat16), (("row", 1), ("col", 2)), half).astype(
        grad_mixed.dtype
    )
    grad_image = (
        cotangent.astype(jnp.float32)
        + backward_taps(grad_pad, depth_kernel, KSIZE, tile_rows, tile_cols)
    ).astype(jnp.bfloat16)
    grad_kernel = kernel_grad(grad_mixed, padded, KSIZE, tile_rows, tile_cols)
    totals = lax.psum(
        (grad_kernel, grad_gain, grad_shift, grad_exp, grad_off, grad_red), ("row", "col")
    )
    pixels_all = pixels * lax.axis_size("row") * lax.axis_size("col")
    scale = float(pixels_all) ** (-0.5)
    return (
        result,
        grad_image,
        totals[0] * scale,
        totals[1] * scale,
        totals[2] * scale,
        totals[3] * scale,
        totals[4] * scale,
        totals[5] * scale,
    )


def solution(mesh):
    in_specs = (
        P("ch", "row", "col"),
        P("ch", None),
        P("ch"),
        P("ch"),
        P(None, "ch"),
        P(),
        P("ch", None),
        P("ch", "row", "col"),
    )
    out_specs = (
        P("ch", "row", "col"),
        P("ch", "row", "col"),
        P("ch", None),
        P("ch"),
        P("ch"),
        P(None, "ch"),
        P("ch"),
        P("ch", None),
    )
    return jax.shard_map(body, mesh=mesh, in_specs=in_specs, out_specs=out_specs, check_vma=False)
```

profile of v0, /device:TPU:1, one launch (start us, length us, event | category | flops | bytes accessed | tf_op | source)
XLA Modules:
  0.0 1113.7 jit_solution(2712978404241594079)
XLA Ops:
  8.1 1.0 fusion.13
  9.0 4.6 collective-permute-start
  13.6 5.5 collective-permute-start.1
  20.3 2.8 collective-permute-start.2
  23.1 1.3 collective-permute-start.3
  24.4 10.6 all_gather.7
  36.5 57.9 %while.48 = (s32[]{:T(128)}, f32[64,4,128]{2,1,0:T(4,128)S(1)}, f32[64,49]{0,1:T(8,128)}, f32[64,10,134]{2,1,0:T(8,128)S(1)}, s32[]{:T(128)}, /*index=5*/s32[]{:T(128)}, s32[]{:T(128)}, s32[]{:T(128)}, s32[]{:T(128)}, s32[]{:T(128)}) while((s32[]{:T(128)}, f32[64,4,128]{2,1,0:T(4,128)S(1)}, f32[64,49]{0,1:T(8,128)}, ...), condition=%wide.region_1.2_spmd.clone, body=%wide.region_0.1_spmd.clone.sunk | while | flops 98325 | bytes 394290 | solution.py:61
  94.4 7.8 psum.70
  102.4 6.0 psum.71
  109.3 10.1 all_gather.6
  119.6 1.1 fusion.8
  123.7 1.0 copy.25
  124.7 346.0 %all-reduce.5.cloned.1.call-done = (f32[256,256]{1,0:T(8,128)}, f32[256,256]{1,0:T(8,128)}) async-done(((f32[256,256]{1,0:T(8,128)}, f32[256,256]{1,0:T(8,128)}), (f32[256,256]{1,0:T(8,128)}, f32[256,256]{1,0:T(8,128)})) %all-reduce.5.cloned.1.call-update) | async-done | bytes 524304 | tf_op jit(solution)/shard_map/psum | solution.py:155
  470.8 1.9 broadcast_multiply_fusion
  472.6 1.0 copy.28
  474.4 8.4 all-reduce.2
  482.9 50.7 %while.47 = (s32[]{:T(128)}, f32[64,49]{0,1:T(8,128)S(1)}, f32[64,10,134]{2,1,0:T(8,128)S(1)}, f32[64,4,128]{2,1,0:T(4,128)S(1)}, s32[]{:T(128)}, /*index=5*/s32...) while((s32[]{:T(128)}, f32[64,49]{0,1:T(8,128)S(1)}, f32[64,10,134]{2,1,0:T(8,128)S(1)}, ...), condition=%wide.region_16.17_spmd, body=%wide.region_14.16_spmd.sunk | while | flops 65492 | bytes 263208 | solution.py:90
  483.0 0.9 multiply_reduce_fusion.6
  484.0 0.9 multiply_reduce_fusion.6
  485.1 0.9 multiply_reduce_fusion.6
  486.1 0.9 multiply_reduce_fusion.6
  487.1 0.9 multiply_reduce_fusion.6
  488.2 0.9 multiply_reduce_fusion.6
  489.2 0.9 multiply_reduce_fusion.6
  490.2 0.9 multiply_reduce_fusion.6
  491.3 0.9 multiply_reduce_fusion.6
  492.3 0.9 multiply_reduce_fusion.6
  493.3 0.9 multiply_reduce_fusion.6
  494.4 0.9 multiply_reduce_fusion.6
  495.4 0.9 multiply_reduce_fusion.6
  496.5 0.9 multiply_reduce_fusion.6
  497.5 0.9 multiply_reduce_fusion.6
  498.5 0.9 multiply_reduce_fusion.6
  499.6 0.9 multiply_reduce_fusion.6
  500.6 0.9 multiply_reduce_fusion.6
  501.6 0.9 multiply_reduce_fusion.6
  502.7 0.9 multiply_reduce_fusion.6
  503.7 0.9 multiply_reduce_fusion.6
  504.7 0.9 multiply_reduce_fusion.6
  505.8 0.9 multiply_reduce_fusion.6
  506.8 0.9 multiply_reduce_fusion.6
  507.8 0.9 multiply_reduce_fusion.6
  508.9 0.9 multiply_reduce_fusion.6
  509.9 0.9 multiply_reduce_fusion.6
  510.9 0.9 multiply_reduce_fusion.6
  512.0 0.9 multiply_reduce_fusion.6
  513.0 0.9 multiply_reduce_fusion.6
  516.1 0.9 multiply_reduce_fusion.6
  517.1 0.9 multiply_reduce_fusion.6
  522.3 0.9 multiply_reduce_fusion.6
  523.4 0.9 multiply_reduce_fusion.6
  524.4 0.9 multiply_reduce_fusion.6
  528.5 0.9 multiply_reduce_fusion.6
  529.6 0.9 multiply_reduce_fusion.6
  530.6 0.9 multiply_reduce_fusion.6
  533.7 477.5 %all-reduce = (f32[64,49]{0,1:T(8,128)S(1)}, f32[64]{0:T(128)S(1)}, f32[64]{0:T(128)S(1)}, f32[256]{0:T(256)S(1)}) all-reduce(f32[64,49]{0,1:T(8,128)S(1)} %get-tuple-element.351, f32[64]{0:T(128)S(1)} %get-tuple-element.382, f32[64]{0:T(128)S(1)} %get-tuple-element.384, ...), channel_id=1, replica_groups=mesh['row'=8,'col'=16,'ch'=4] {'row','col'}, use_global_device_ids=true, to_apply=%region_17.18 | all-reduce | flops 3520 | bytes 28160 | tf_op jit(solution)/shard_map/psum | solution.py:155
  1012.4 1.9 collective-permute-start.4
  1014.3 19.1 %collective-permute-start.5 = (bf16[64,3,128]{2,1,0:T(4,128)(2,1)S(1)}, bf16[64,3,128]{2,1,0:T(4,128)(2,1)S(1)}, u32[]{:S(2)}, u32[]{:S(2)}) collective-permute-start(bf16[64,3,128]{2,1,0:T(4,128)(2,1)S(1)} %get-tuple-element.425), channel_id=1, source_target_pairs={{64,0},{128,64},{192,128},{256,192},{320,256},{384,320},{448,384},... | collective-permute-start | bytes 147464 | tf_op jit(solution)/shard_map/ppermute | solution.py:20
  1034.6 1.3 collective-permute-start.6
  1035.9 1.3 collective-permute-start.7
  1037.7 3.5 collective-permute-done.6
  1041.2 3.8 collective-permute-done.7
  1045.8 57.9 %while.49 = (s32[]{:T(128)}, f32[64,4,128]{2,1,0:T(4,128)S(1)}, f32[64,49]{0,1:T(8,128)}, f32[64,10,134]{2,1,0:T(8,128)S(1)}, s32[]{:T(128)}, /*index=5*/s32[]{:...) while((s32[]{:T(128)}, f32[64,4,128]{2,1,0:T(4,128)S(1)}, ...), condition=%wide.region_13.14_spmd.clone, body=%wide.region_12.13_spmd.clone.sunk | while | flops 98327 | bytes 394322 | solution.py:74
  1104.4 1.0 copy.26
  (318 shorter events, 135.5 us)
Async XLA Ops:
  8.0 112.7 %copy-start = (bf16[256,256]{1,0:T(8,128)(2,1)S(1)}, bf16[256,256]{1,0:T(8,128)(2,1)}, u32[]{:S(2)}) copy-start(bf16[256,256]{1,0:T(8,128)(2,1)} %param.20) | copy-start | bytes 393220
  8.0 11.1 copy-start.3
  8.0 462.7 %all-reduce.5.cloned.1.call-start = ((), (), s32[]{:S(2)}) async-start(), calls=%async_computation.4 | async-start | bytes 1048576 | tf_op jit(solution)/shard_map/psum | solution.py:155
  9.0 10.1 collective-permute-start
  13.6 6.3 collective-permute-start.1
  19.1 0.9 copy-start.1
  20.3 15.5 %collective-permute-start.2 = (bf16[64,10,3]{2,1,0:T(8,128)(2,1)S(1)}, bf16[64,10,3]{2,1,0:T(8,128)(2,1)S(1)}, u32[]{:S(2)}, u32[]{:S(2)}) collective-permute-start(bf16[64,10,3]{2,1,0:T(8,128)(2,1)S(1)} %get-tuple-element.422), channel_id=1, source_target_pairs={{0,4},{4,8},{8,12},{12,16},{16,20},{20,24},{24,28},{28,32},{32,36}... | collective-permute-start | bytes 11528 | tf_op jit(solution)/shard_map/ppermute | solution.py:19
  23.1 12.7 %collective-permute-start.3 = (bf16[64,10,3]{2,1,0:T(8,128)(2,1)S(1)}, bf16[64,10,3]{2,1,0:T(8,128)(2,1)S(1)}, u32[]{:S(2)}, u32[]{:S(2)}) collective-permute-start(bf16[64,10,3]{2,1,0:T(8,128)(2,1)S(1)} %get-tuple-element.423), channel_id=1, source_target_pairs={{4,0},{8,4},{12,8},{16,12},{20,16},{24,20},{28,24},{32,28},{36,32}... | collective-permute-start | bytes 11528 | tf_op jit(solution)/shard_map/ppermute | solution.py:20
  108.4 0.7 copy-start.4
  108.4 0.7 copy-start.5
  109.3 10.1 copy-start.2
  122.1 350.5 %reduce-scatter.9.cloned.1.call-start = ((), (), s32[]{:S(2)}) async-start(), calls=%async_computation.3 | async-start | bytes 327680
  123.3 981.1 %reduce-scatter.7.cloned.1.call-start = ((), (), s32[]{:S(2)}) async-start(), calls=%async_computation.2 | async-start | bytes 655360
  1012.4 21.6 %collective-permute-start.4 = (bf16[64,3,128]{2,1,0:T(4,128)(2,1)S(1)}, bf16[64,3,128]{2,1,0:T(4,128)(2,1)S(1)}, u32[]{:S(2)}, u32[]{:S(2)}) collective-permute-start(bf16[64,3,128]{2,1,0:T(4,128)(2,1)S(1)} %get-tuple-element.424), channel_id=1, source_target_pairs={{0,64},{64,128},{128,192},{192,256},{256,320},{320,384},{384,448},... | collective-permute-start | bytes 147464 | tf_op jit(solution)/shard_map/ppermute | solution.py:19
  1014.3 20.0 %collective-permute-start.5 = (bf16[64,3,128]{2,1,0:T(4,128)(2,1)S(1)}, bf16[64,3,128]{2,1,0:T(4,128)(2,1)S(1)}, u32[]{:S(2)}, u32[]{:S(2)}) collective-permute-start(bf16[64,3,128]{2,1,0:T(4,128)(2,1)S(1)} %get-tuple-element.425), channel_id=1, source_target_pairs={{64,0},{128,64},{192,128},{256,192},{320,256},{384,320},{448,384},... | collective-permute-start | bytes 147464 | tf_op jit(solution)/shard_map/ppermute | solution.py:20
  1034.6 6.7 collective-permute-start.6
  1035.9 9.2 collective-permute-start.7
Sparse Core Ops, SparseCore 0:
  122.3 348.4 all-reduce.4
Sparse Core Ops, SparseCore 1:
  125.4 38.8 reduce-scatter.8
  167.0 28.9 reduce-scatter.6
where the time goes:
time: 1120 us; the launch traced here: 1110 us
  blocking collectives  520 us (46%)
  waiting for transfers between devices  355 us (32%)
  other arithmetic  97.2 us (9%)
  local copies, waits for them, and re-layouts  76.4 us (7%)
  starting transfers between devices  37.9 us (3%)
  between operations  15.7 us (1%)
    psum x1, blocking collectives, body(): lax.psum((grad_kernel, grad_gain, grad_shift, grad_exp, grad_off, grad_re...  477 us
    psum x1, waiting for transfers between devices, body(): lax.psum((grad_kernel, grad_gain, grad_shift, grad_exp, grad_off, grad_re...  346 us
    mul x98, local copies, waits for them, and re-layouts, tap_window(): return weight[:, :, None] * window  68.2 us
    reduce_sum x49, other arithmetic, kernel_step(): column = jnp.sum(grad_mixed * window, axis=(1, 2))  46.4 us
    ppermute x4, starting transfers between devices, padded_2(): after = lax.ppermute(leading, axis, down)  27.1 us
  transfers between devices with their start and end apart: 11, of which 5 were waited for; matrix products, arithmetic and copies ran while one was open for 10% of the time, Pallas kernels for 0%

commit v1 on v0

--- a/solution.py
+++ b/solution.py
@@ -7,6 +7,7 @@
 epsilon = 1e-06
 root_two_pi = 0.7978845608028654
 cubic_coef = 0.044715
+take_the_masks = lambda x0: jax.lax.psum(jax.lax.psum(x0, "col"), "row")
 
 
 def padded_2(x, sides, width):
@@ -152,9 +153,7 @@
         + backward_taps(grad_pad, depth_kernel, KSIZE, tile_rows, tile_cols)
     ).astype(jnp.bfloat16)
     grad_kernel = kernel_grad(grad_mixed, padded, KSIZE, tile_rows, tile_cols)
-    totals = lax.psum(
-        (grad_kernel, grad_gain, grad_shift, grad_exp, grad_off, grad_red), ("row", "col")
-    )
+    totals = take_the_masks((grad_kernel, grad_gain, grad_shift, grad_exp, grad_off, grad_red))
     pixels_all = pixels * lax.axis_size("row") * lax.axis_size("col")
     scale = float(pixels_all) ** (-0.5)
     return (

time: 1120 us -> 509 us (0.45)
  blocking collectives: 520 us -> 130 us
  waiting for transfers between devices: 355 us -> 150 us
  starting transfers between devices: 37.9 us -> 23.6 us
    psum x1 -> x2, blocking collectives: 477 us -> 87.2 us  [take_the_masks = lambda x0: jax.lax.psum(jax.lax.psum(x0, 'col'), 'row')]
    psum x1 -> x2, waiting for transfers between devices: 346 us -> 140 us  [take_the_masks = lambda x0: jax.lax.psum(jax.lax.psum(x0, 'col'), 'row')]
    ppermute x4, starting transfers between devices: 27.1 us -> 11.2 us  [padded_2(): after = lax.ppermute(leading, axis, down)]
  transfers between devices with their start and end apart: 11 -> 12, of which waited for: 5 -> 5; matrix products, arithmetic and copies ran while one was open for 10% -> 23% of each run, Pallas kernels for 0% -> 0%
where the time goes in v1:
time: 509 us; the launch traced here: 504 us
  waiting for transfers between devices  150 us (29%)
  blocking collectives  130 us (26%)
  other arithmetic  97.2 us (19%)
  local copies, waits for them, and re-layouts  76.4 us (15%)
  starting transfers between devices  23.6 us (5%)
  between operations  15.8 us (3%)
  loops' own time  8.1 us (2%)
    psum x2, waiting for transfers between devices, take_the_masks = lambda x0: jax.lax.psum(jax.lax.psum(x0, 'col'), 'row')  140 us
    psum x2, blocking collectives, take_the_masks = lambda x0: jax.lax.psum(jax.lax.psum(x0, 'col'), 'row')  87.2 us
    mul x98, local copies, waits for them, and re-layouts, tap_window(): return weight[:, :, None] * window  68.2 us
    reduce_sum x49, other arithmetic, kernel_step(): column = jnp.sum(grad_mixed * window, axis=(1, 2))  46.4 us
    add x49, other arithmetic, backward_step(): accum + tap_window(padded, kernel, tap, first, second, tile_rows, tile_cols)  21.2 us
    add x49, other arithmetic, forward_step(): accum + tap_window(padded, kernel, tap, first, second, tile_rows, tile_cols)  21.2 us
    ppermute x4, starting transfers between devices, padded_2(): before = lax.ppermute(last, axis, up)  12.3 us
    ppermute x4, starting transfers between devices, padded_2(): after = lax.ppermute(leading, axis, down)  11.2 us
  transfers between devices with their start and end apart: 12, of which 5 were waited for; matrix products, arithmetic and copies ran while one was open for 23% of the time, Pallas kernels for 0%

profile of v1, /device:TPU:1, one launch (start us, length us, event | category | flops | bytes accessed | tf_op | source)
XLA Modules:
  0.0 504.4 jit_solution(5220785638814562400)
XLA Ops:
  8.1 1.0 fusion.13
  9.0 4.6 collective-permute-start
  13.6 5.5 %collective-permute-start.1 = (bf16[64,3,128]{2,1,0:T(4,128)(2,1)S(1)}, bf16[64,3,128]{2,1,0:T(4,128)(2,1)S(1)}, u32[]{:S(2)}, u32[]{:S(2)}) collective-permute-start(bf16[64,3,128]{2,1,0:T(4,128)(2,1)S(1)} %get-tuple-element.433), channel_id=1, source_target_pairs={{64,0},{128,64},{192,128},{256,192},{320,256},{384,320},{448,384},... | collective-permute-start | bytes 147464 | tf_op jit(solution)/shard_map/ppermute | solution.py:21
  20.3 2.8 collective-permute-start.2
  23.1 1.3 collective-permute-start.3
  24.4 10.6 %all_gather.7 = bf16[256,512]{1,0:T(8,128)(2,1)S(1)} all-gather(bf16[64,512]{1,0:T(8,128)(2,1)S(1)} %bitcast.43), channel_id=1, replica_groups=mesh['row'=8,'col'=16,'ch'=4] {'ch'}, dimensions={0}, use_global_device_ids=true | all-gather | bytes 327680 | tf_op jit(solution)/shard_map/all_gather | solution.py:123
  36.5 57.9 %while.48 = (s32[]{:T(128)}, f32[64,4,128]{2,1,0:T(4,128)S(1)}, f32[64,49]{0,1:T(8,128)}, f32[64,10,134]{2,1,0:T(8,128)S(1)}, s32[]{:T(128)}, /*index=5*/s32[]{:T(128)}, s32[]{:T(128)}, s32[]{:T(128)}, s32[]{:T(128)}, s32[]{:T(128)}) while((s32[]{:T(128)}, f32[64,4,128]{2,1,0:T(4,128)S(1)}, f32[64,49]{0,1:T(8,128)}, ...), condition=%wide.region_1.2_spmd.clone, body=%wide.region_0.1_spmd.clone.sunk | while | flops 98325 | bytes 394290 | solution.py:62
  94.4 7.8 %psum.112 = f32[4,128]{1,0:T(4,128)S(1)} all-reduce(f32[4,128]{1,0:T(4,128)S(1)} %reduce_sum.81), channel_id=1, replica_groups=mesh['row'=8,'col'=16,'ch'=4] {'ch'}, use_global_device_ids=true, to_apply=%region_3.4 | all-reduce | flops 512 | bytes 4096 | tf_op jit(solution)/shard_map/psum | solution.py:108
  102.4 6.0 %psum.113 = f32[4,128]{1,0:T(4,128)S(1)} all-reduce(f32[4,128]{1,0:T(4,128)S(1)} %multiply_reduce_fusion.4), channel_id=1, replica_groups=mesh['row'=8,'col'=16,'ch'=4] {'ch'}, use_global_device_ids=true, to_apply=%region_5.6 | all-reduce | flops 512 | bytes 4096 | tf_op jit(solution)/shard_map/psum | solution.py:110
  109.3 10.1 %all_gather.6 = bf16[256,512]{1,0:T(8,128)(2,1)S(1)} all-gather(bf16[64,512]{1,0:T(8,128)(2,1)S(1)} %bitcast.44), channel_id=1, replica_groups=mesh['row'=8,'col'=16,'ch'=4] {'ch'}, dimensions={0}, use_global_device_ids=true | all-gather | bytes 327680 | tf_op jit(solution)/shard_map/all_gather | solution.py:116
  119.6 1.1 fusion.8
  123.4 139.6 %all-reduce.8.cloned.1.call-done = (f32[256,256]{1,0:T(8,128)}, f32[256,256]{1,0:T(8,128)}) async-done(((f32[256,256]{1,0:T(8,128)}, f32[256,256]{1,0:T(8,128)}), (f32[256,256]{1,0:T(8,128)}, f32[256,256]{1,0:T(8,128)})) %all-reduce.8.cloned.1.call-update) | async-done | bytes 524304 | tf_op jit(solution)/shard_map/psum | solution.py:10
  263.4 1.0 copy.25
  264.4 1.0 copy.28
  266.2 8.4 %all-reduce.4 = (f32[4,128]{1,0:T(4,128)S(1)}, f32[4,128]{1,0:T(4,128)S(1)}) all-reduce(f32[4,128]{1,0:T(4,128)S(1)} %get-tuple-element.383, f32[4,128]{1,0:T(4,128)S(1)} %bitcast.48), channel_id=1, replica_groups=mesh['row'=8,'col'=16,'ch'=4] {'ch'}, use_global_device_ids=true, to_apply=%region_11.12 | all-reduce | flops 1024 | bytes 8192 | tf_op jit(solution)/shard_map/psum | solution.py:137
  274.8 50.7 %while.47 = (s32[]{:T(128)}, f32[64,49]{0,1:T(8,128)S(1)}, f32[64,10,134]{2,1,0:T(8,128)S(1)}, f32[64,4,128]{2,1,0:T(4,128)S(1)}, s32[]{:T(128)}, /*index=5*/s32...) while((s32[]{:T(128)}, f32[64,49]{0,1:T(8,128)S(1)}, f32[64,10,134]{2,1,0:T(8,128)S(1)}, ...), condition=%wide.region_16.17_spmd, body=%wide.region_14.16_spmd.sunk | while | flops 65492 | bytes 263208 | solution.py:91
  274.8 0.9 multiply_reduce_fusion.6
  275.8 0.9 multiply_reduce_fusion.6
  276.9 0.9 multiply_reduce_fusion.6
  277.9 0.9 multiply_reduce_fusion.6
  279.0 0.9 multiply_reduce_fusion.6
  280.0 0.9 multiply_reduce_fusion.6
  281.0 0.9 multiply_reduce_fusion.6
  282.1 0.9 multiply_reduce_fusion.6
  283.1 0.9 multiply_reduce_fusion.6
  284.1 0.9 multiply_reduce_fusion.6
  285.2 0.9 multiply_reduce_fusion.6
  286.2 0.9 multiply_reduce_fusion.6
  287.2 0.9 multiply_reduce_fusion.6
  288.3 0.9 multiply_reduce_fusion.6
  289.3 0.9 multiply_reduce_fusion.6
  290.3 0.9 multiply_reduce_fusion.6
  291.4 0.9 multiply_reduce_fusion.6
  292.4 0.9 multiply_reduce_fusion.6
  293.4 0.9 multiply_reduce_fusion.6
  294.5 0.9 multiply_reduce_fusion.6
  295.5 0.9 multiply_reduce_fusion.6
  296.5 0.9 multiply_reduce_fusion.6
  297.6 0.9 multiply_reduce_fusion.6
  298.6 0.9 multiply_reduce_fusion.6
  299.6 0.9 multiply_reduce_fusion.6
  300.7 0.9 multiply_reduce_fusion.6
  302.8 0.9 multiply_reduce_fusion.6
  303.8 0.9 multiply_reduce_fusion.6
  309.0 0.9 multiply_reduce_fusion.6
  310.0 0.9 multiply_reduce_fusion.6
  311.0 0.9 multiply_reduce_fusion.6
  315.2 0.9 multiply_reduce_fusion.6
  316.2 0.9 multiply_reduce_fusion.6
  317.2 0.9 multiply_reduce_fusion.6
  322.4 0.9 multiply_reduce_fusion.6
  323.4 0.9 multiply_reduce_fusion.6
  325.5 40.5 %all-reduce = (f32[64,49]{0,1:T(8,128)S(1)}, f32[64]{0:T(128)S(1)}, f32[64]{0:T(128)S(1)}, f32[256]{0:T(256)S(1)}) all-reduce(f32[64,49]{0,1:T(8,128)S(1)} %get-tuple-element.351, f32[64]{0:T(128)S(1)} %get-tuple-element.382, f32[64]{0:T(128)S(1)} %get-tuple-element.384, ...), channel_id=1, replica_groups=mesh['row'=8,'col'=16,'ch'=4] {'col'}, use_global_device_ids=true, to_apply=%region_17.18 | all-reduce | flops 3520 | bytes 28160 | tf_op jit(solution)/shard_map/psum | solution.py:10
  366.0 46.7 %all-reduce.2 = (f32[64,49]{0,1:T(8,128)S(1)}, f32[64]{0:T(128)S(1)}, f32[64]{0:T(128)S(1)}, f32[256]{0:T(256)S(1)}) all-reduce(f32[64,49]{0,1:T(8,128)S(1)} %get-tuple-element.410, f32[64]{0:T(128)S(1)} %get-tuple-element.411, f32[64]{0:T(128)S(1)} %get-tuple-element.412, ...), channel_id=1, replica_groups=mesh['row'=8,'col'=16,'ch'=4] {'row'}, use_global_device_ids=true, to_apply=%region_18.19 | all-reduce | flops 3520 | bytes 28160 | tf_op jit(solution)/shard_map/psum | solution.py:10
  413.9 3.6 collective-permute-start.4
  417.5 3.1 collective-permute-start.5
  421.2 1.9 collective-permute-done.5
  423.4 1.3 collective-permute-start.6
  424.7 1.3 collective-permute-start.7
  426.6 3.2 collective-permute-done.6
  429.8 4.1 collective-permute-done.7
  434.6 57.9 %while.49 = (s32[]{:T(128)}, f32[64,4,128]{2,1,0:T(4,128)S(1)}, f32[64,49]{0,1:T(8,128)}, f32[64,10,134]{2,1,0:T(8,128)S(1)}, s32[]{:T(128)}, /*index=5*/s32[]{:...) while((s32[]{:T(128)}, f32[64,4,128]{2,1,0:T(4,128)S(1)}, ...), condition=%wide.region_13.14_spmd.clone, body=%wide.region_12.13_spmd.clone.sunk | while | flops 98327 | bytes 394322 | solution.py:75
  493.2 1.9 broadcast_multiply_fusion
  495.1 1.0 copy.26
  (322 shorter events, 137.1 us)
Async XLA Ops:
  8.0 112.7 %copy-start = (bf16[256,256]{1,0:T(8,128)(2,1)S(1)}, bf16[256,256]{1,0:T(8,128)(2,1)}, u32[]{:S(2)}) copy-start(bf16[256,256]{1,0:T(8,128)(2,1)} %param.20) | copy-start | bytes 393220
  8.0 11.1 %copy-start.3 = (bf16[64,4,128]{2,1,0:T(4,128)(2,1)S(1)}, bf16[64,4,128]{2,1,0:T(4,128)(2,1)}, u32[]{:S(2)}) copy-start(bf16[64,4,128]{2,1,0:T(4,128)(2,1)} %param.21) | copy-start | bytes 196612
  8.0 254.9 %all-reduce.8.cloned.1.call-start = ((), (), s32[]{:S(2)}) async-start(), calls=%async_computation.4 | async-start | bytes 1048576 | tf_op jit(solution)/shard_map/psum | solution.py:10
  9.0 10.1 %collective-permute-start = (bf16[64,3,128]{2,1,0:T(4,128)(2,1)S(1)}, bf16[64,3,128]{2,1,0:T(4,128)(2,1)S(1)}, u32[]{:S(2)}, u32[]{:S(2)}) collective-permute-start(bf16[64,3,128]{2,1,0:T(4,128)(2,1)S(1)} %get-tuple-element.432), channel_id=1, source_target_pairs={{0,64},{64,128},{128,192},{192,256},{256,320},{320,384},{384,448},... | collective-permute-start | bytes 147464 | tf_op jit(solution)/shard_map/ppermute | solution.py:20
  13.6 6.3 %collective-permute-start.1 = (bf16[64,3,128]{2,1,0:T(4,128)(2,1)S(1)}, bf16[64,3,128]{2,1,0:T(4,128)(2,1)S(1)}, u32[]{:S(2)}, u32[]{:S(2)}) collective-permute-start(bf16[64,3,128]{2,1,0:T(4,128)(2,1)S(1)} %get-tuple-element.433), channel_id=1, source_target_pairs={{64,0},{128,64},{192,128},{256,192},{320,256},{384,320},{448,384},... | collective-permute-start | bytes 147464 | tf_op jit(solution)/shard_map/ppermute | solution.py:21
  19.1 0.9 copy-start.1
  20.3 15.5 %collective-permute-start.2 = (bf16[64,10,3]{2,1,0:T(8,128)(2,1)S(1)}, bf16[64,10,3]{2,1,0:T(8,128)(2,1)S(1)}, u32[]{:S(2)}, u32[]{:S(2)}) collective-permute-start(bf16[64,10,3]{2,1,0:T(8,128)(2,1)S(1)} %get-tuple-element.428), channel_id=1, source_target_pairs={{0,4},{4,8},{8,12},{12,16},{16,20},{20,24},{24,28},{28,32},{32,36}... | collective-permute-start | bytes 11528 | tf_op jit(solution)/shard_map/ppermute | solution.py:20
  23.1 12.7 %collective-permute-start.3 = (bf16[64,10,3]{2,1,0:T(8,128)(2,1)S(1)}, bf16[64,10,3]{2,1,0:T(8,128)(2,1)S(1)}, u32[]{:S(2)}, u32[]{:S(2)}) collective-permute-start(bf16[64,10,3]{2,1,0:T(8,128)(2,1)S(1)} %get-tuple-element.429), channel_id=1, source_target_pairs={{4,0},{8,4},{12,8},{16,12},{20,16},{24,20},{28,24},{32,28},{36,32}... | collective-permute-start | bytes 11528 | tf_op jit(solution)/shard_map/ppermute | solution.py:21
  108.4 0.7 copy-start.4
  108.4 0.7 copy-start.5
  109.3 10.1 %copy-start.2 = (bf16[256,256]{1,0:T(8,128)(2,1)S(1)}, bf16[256,256]{1,0:T(8,128)(2,1)}, u32[]{:S(2)}) copy-start(bf16[256,256]{1,0:T(8,128)(2,1)} %param.18) | copy-start | bytes 393220
  122.1 142.3 %reduce-scatter.9.cloned.1.call-start = ((), (), s32[]{:S(2)}) async-start(), calls=%async_computation.3 | async-start | bytes 327680
  123.3 369.9 %all-reduce.10.cloned.1.call-start = ((), (), s32[]{:S(2)}) async-start(), calls=%async_computation.5 | async-start | bytes 1048576 | tf_op jit(solution)/shard_map/psum | solution.py:10
  263.0 232.1 %reduce-scatter.7.cloned.1.call-start = ((), (), s32[]{:S(2)}) async-start(), calls=%async_computation.2 | async-start | bytes 655360
  413.9 7.3 %collective-permute-start.4 = (bf16[64,3,128]{2,1,0:T(4,128)(2,1)S(1)}, bf16[64,3,128]{2,1,0:T(4,128)(2,1)S(1)}, u32[]{:S(2)}, u32[]{:S(2)}) collective-permute-start(bf16[64,3,128]{2,1,0:T(4,128)(2,1)S(1)} %get-tuple-element.430), channel_id=1, source_target_pairs={{0,64},{64,128},{128,192},{192,256},{256,320},{320,384},{384,448},... | collective-permute-start | bytes 147464 | tf_op jit(solution)/shard_map/ppermute | solution.py:20
  417.5 5.6 %collective-permute-start.5 = (bf16[64,3,128]{2,1,0:T(4,128)(2,1)S(1)}, bf16[64,3,128]{2,1,0:T(4,128)(2,1)S(1)}, u32[]{:S(2)}, u32[]{:S(2)}) collective-permute-start(bf16[64,3,128]{2,1,0:T(4,128)(2,1)S(1)} %get-tuple-element.431), channel_id=1, source_target_pairs={{64,0},{128,64},{192,128},{256,192},{320,256},{384,320},{448,384},... | collective-permute-start | bytes 147464 | tf_op jit(solution)/shard_map/ppermute | solution.py:21
  423.4 6.4 %collective-permute-start.6 = (bf16[64,10,3]{2,1,0:T(8,128)(2,1)S(1)}, bf16[64,10,3]{2,1,0:T(8,128)(2,1)S(1)}, u32[]{:S(2)}, u32[]{:S(2)}) collective-permute-start(bf16[64,10,3]{2,1,0:T(8,128)(2,1)S(1)} %get-tuple-element.426), channel_id=1, source_target_pairs={{0,4},{4,8},{8,12},{12,16},{16,20},{20,24},{24,28},{28,32},{32,36}... | collective-permute-start | bytes 11528 | tf_op jit(solution)/shard_map/ppermute | solution.py:20
  424.7 9.2 %collective-permute-start.7 = (bf16[64,10,3]{2,1,0:T(8,128)(2,1)S(1)}, bf16[64,10,3]{2,1,0:T(8,128)(2,1)S(1)}, u32[]{:S(2)}, u32[]{:S(2)}) collective-permute-start(bf16[64,10,3]{2,1,0:T(8,128)(2,1)S(1)} %get-tuple-element.427), channel_id=1, source_target_pairs={{4,0},{8,4},{12,8},{16,12},{20,16},{24,20},{28,24},{32,28},{36,32}... | collective-permute-start | bytes 11528 | tf_op jit(solution)/shard_map/ppermute | solution.py:21
Sparse Core Ops, SparseCore 0:
  122.3 140.6 all-reduce.7
  265.4 81.5 all-reduce.9
Sparse Core Ops, SparseCore 1:
  126.0 38.7 reduce-scatter.8
  266.3 33.2 reduce-scatter.6
